TPU v7x, 512 devices: a whole 4x8x8 slice. The times are simulated.
512 devices in a mesh: section: 16 (over z_lo, y), shard: 32 (over x, z_hi, core).
Axes of the slice: x: 4, y: 8, z: 8 (z_hi: 4, z_lo: 2; z = z_hi * 2 + z_lo), core: 2. Of those that a mesh axis runs over, the one named last changes fastest.
Arguments:
- layer_input: bfloat16 [16, 4096, 3072], P('section', 'shard'), may hold values from -150 to 150
- out_grad: bfloat16 [16, 4096, 3072], P('section', 'shard'), may hold values from -60 to 60
- modulation: float32 [16, 4, 3, 3072], P('section'), may hold values from -3 to 3
- proj_weight: bfloat16 [16, 3072, 3072], P('section', 'shard'), may hold values from -0.109375 to 0.109375
Outputs:
- handoff: bfloat16 [16, 4096, 3072], P('section', 'shard')
- mod_grad: float32 [16, 4, 3, 3072], P('section')
All inputs are finite; a program needn't handle non-finite values.
Results may differ from a plain program's by a relative error of at most 0.0029.
Values may be sent and summed in bfloat16 or wider, within the bound.
A program may use at most 128 MiB of HBM per device.

v0:
```python
import jax
import jax.numpy as jnp
from jax import lax
from jax.sharding import PartitionSpec as P

SEQS = 4


def swapped(value, axis, apart):
    mask = 2**apart
    pairs = [(source, source ^ mask) for source in range(lax.axis_size(axis))]
    return lax.ppermute(value, axis, pairs)


def passed_along(value, axis, steps):
    count = lax.axis_size(axis)
    leading, last = (max(0, -steps), min(count, count - steps))
    return lax.ppermute(value, axis, [(source, source + steps) for source in range(leading, last)])


def select_rows(token_ids, seq_length):
    sample = token_ids // seq_length
    return (sample[:, None] == jnp.arange(SEQS, dtype=jnp.int32)[None, :]).astype(jnp.float32)


def norm_rows(activation):
    values = activation.astype(jnp.float32)
    center = values - jnp.mean(values, axis=-1, keepdims=True)
    variance = jnp.mean(center * center, axis=-1, keepdims=True)
    inv_scale = lax.rsqrt(variance + 1e-06)
    return (center * inv_scale, inv_scale)


def on_device(layer_input, out_grad, modulation, proj_weight):
    shard_count = lax.axis_size("shard")
    my_index = lax.axis_index("shard")
    group_bits = 1
    group_size = 2**group_bits
    own_input = layer_input[0]
    own_grad = out_grad[0]
    mod_table = modulation[0]
    weight_rows = proj_weight[0]
    row_count, feat_count = own_input.shape
    col_count = feat_count // group_size
    seq_length = row_count * shard_count // SEQS
    position = my_index % group_size
    own_sample = my_index * row_count // seq_length
    own_mod = lax.dynamic_index_in_dim(mod_table, own_sample, 0, keepdims=False)
    sample_hot = (jnp.arange(SEQS, dtype=jnp.int32) == own_sample).astype(jnp.float32)
    normed, inv_scale = norm_rows(own_input)
    modulated = (normed * (1.0 + own_mod[1]) + own_mod[0]).astype(jnp.bfloat16)
    joined = jnp.stack([modulated, own_grad], axis=0)
    bit_number = 0
    partner = swapped(joined, "shard", bit_number)
    upper_side = my_index // 2**bit_number % 2 == 1
    lower_part = jnp.where(upper_side, partner, joined)
    upper_part = jnp.where(upper_side, joined, partner)
    joined = jnp.concatenate([lower_part, upper_part], axis=1)
    group_input = joined[0]
    group_grad = joined[1]
    piece_rows = weight_rows.shape[0]
    pieces = jnp.transpose(weight_rows.reshape(piece_rows, group_size, col_count), (1, 0, 2))
    outgoing = jnp.broadcast_to(
        pieces[None], (shard_count // group_size, group_size, piece_rows, col_count)
    )
    outgoing = outgoing.reshape(shard_count, piece_rows, col_count)
    incoming = lax.all_to_all(outgoing, "shard", split_axis=0, concat_axis=0, tiled=True)
    weight_cols = incoming.reshape(feat_count, col_count)
    group_ids = (my_index - position) * row_count + jnp.arange(
        group_size * row_count, dtype=jnp.int32
    )
    group_select = select_rows(group_ids, seq_length)
    col_start = position * col_count
    gate_table = lax.dynamic_slice_in_dim(mod_table[:, 2], col_start, col_count, 1)
    gate_cols = jnp.dot(group_select, gate_table, precision=lax.Precision.HIGHEST)
    grad_cols = lax.dynamic_slice_in_dim(group_grad, col_start, col_count, 1).astype(jnp.float32)
    branch = jnp.dot(group_input, weight_cols, preferred_element_type=jnp.float32)
    scaled_grad = (gate_cols * grad_cols).astype(jnp.bfloat16)
    partial_grad = lax.dot_general(
        scaled_grad, weight_cols, (((1,), (1,)), ((), ())), preferred_element_type=jnp.float32
    )
    gate_part = jnp.einsum(
        "rs,rd->sd", group_select, grad_cols * branch, precision=lax.Precision.HIGHEST
    )
    gate_full = lax.dynamic_update_slice(
        jnp.zeros((SEQS, feat_count), jnp.float32), gate_part, (jnp.int32(0), col_start)
    )
    current = partial_grad
    for bit_number in reversed(range(group_bits)):
        half_count = current.shape[0] // 2
        low_half = current[:half_count]
        high_half = current[half_count:]
        upper_side = my_index // 2**bit_number % 2 == 1
        kept_half = jnp.where(upper_side, high_half, low_half)
        sending = jnp.where(upper_side, low_half, high_half)
        current = kept_half + swapped(sending.astype(jnp.bfloat16), "shard", bit_number).astype(
            sending.dtype
        )
    grad_shift = sample_hot[:, None] * jnp.sum(current, axis=0)[None, :]
    grad_scale = sample_hot[:, None] * jnp.sum(current * normed, axis=0)[None, :]
    totals = lax.psum(jnp.stack([grad_shift, grad_scale, gate_full], axis=1), "shard")
    grad_norm = current * (1.0 + own_mod[1])
    centered = grad_norm - jnp.mean(grad_norm, axis=-1, keepdims=True)
    grad_in = own_grad.astype(jnp.float32) + inv_scale * (
        centered - normed * jnp.mean(grad_norm * normed, axis=-1, keepdims=True)
    )
    handoff = passed_along(grad_in.astype(jnp.bfloat16), "section", -1)
    return (handoff[None], totals[None])


def solution(mesh):
    in_specs = (
        P("section", "shard", None),
        P("section", "shard", None),
        P("section", None, None, None),
        P("section", "shard", None),
    )
    out_specs = (P("section", "shard", None), P("section", None, None, None))
    return jax.shard_map(
        on_device, mesh=mesh, in_specs=in_specs, out_specs=out_specs, check_vma=False
    )
```

profile of v0, /device:TPU:1, one launch (start us, length us, event | category | flops | bytes accessed | tf_op | source)
XLA Modules:
  0.0 538.5 jit_solution(8000382200679305160)
XLA Ops:
  7.2 2.2 reshape_squeeze.3
  9.4 4.7 broadcast_in_dim.8
  14.2 14.6 %all-to-all-start = ((bf16[32,96,1536]{2,1,0:T(8,128)(2,1)}), bf16[32,96,1536]{2,1,0:T(8,128)(2,1)}, u32[]{:S(2)}, u32[]{:S(2)}) async-start(bf16[32,96,1536]{2,1,0:T(8,128)(2,1)} %bitcast.61), calls=%async_computation | async-start | bytes 18874368 | tf_op jit(solution)/shard_map/all_to_all | solution.py:67
  28.9 0.2 convert_reduce_fusion
  29.1 0.4 fusion.14
  29.4 0.2 copy-done.9
  29.7 0.4 fusion.18
  30.1 1.3 pad_maximum_fusion.1
  31.4 2.2 collective-permute-start
  33.7 3.4 collective-permute-done
  37.0 1.6 broadcast_select_fusion.1
  38.7 0.3 pad_slice_fusion
  39.0 0.8 copy-done.2
  39.8 0.5 copy-done.4
  40.3 1.2 copy-done.6
  41.5 1.8 fusion
  43.4 144.0 %all-to-all-done = bf16[32,96,1536]{2,1,0:T(8,128)(2,1)} async-done(((bf16[32,96,1536]{2,1,0:T(8,128)(2,1)}), bf16[32,96,1536]{2,1,0:T(8,128)(2,1)}, u32[]{:S(2)}, u32[]{:S(2)}) %all-to-all-start) | async-done | bytes 9437216 | tf_op jit(solution)/shard_map/all_to_all | solution.py:67
  187.4 5.6 %fusion.29 = f32[256,3072]{1,0:T(8,128)S(1)} fusion(bf16[256,1536]{1,0:T(8,128)(2,1)} %fusion, bf16[3072,1536]{1,0:T(8,128)(2,1)} %bitcast.9), kind=kOutput, calls=%fused_computation.59 | convolution fusion | flops 2415919104 | bytes 13369344 | tf_op jit(solution)/shard_map/dot_general | solution.py:79
  192.9 0.1 select_convert_fusion
  193.1 3.7 collective-permute-start.1
  196.9 5.2 convolution_multiply_fusion
  202.1 0.7 fusion.1
  202.8 1.0 fusion.13
  203.8 0.8 fusion.12
  204.5 1.3 collective-permute-start.2
  205.8 0.1 broadcast_multiply_fusion.1
  205.9 0.7 maximum_bitcast_fusion
  206.6 18.9 %collective-permute-done.2 = bf16[128,3072]{1,0:T(8,128)(2,1)S(1)} collective-permute-done((bf16[128,3072]{1,0:T(8,128)(2,1)S(1)}, bf16[128,3072]{1,0:T(8,128)(2,1)S(1)}, u32[]{:S(2)}, u32[]{:S(2)}) %collective-permute-start.2) | collective-permute-done | bytes 786464 | tf_op jit(solution)/shard_map/ppermute | solution.py:18
  225.5 304.5 %all-reduce.2.cloned.1.call-done = f32[1,4,3,3072]{3,1,2,0:T(4,128)} async-done(((f32[1,4,3,3072]{3,1,2,0:T(4,128)}), f32[1,4,3,3072]{3,1,2,0:T(4,128)}) %all-reduce.2.cloned.1.call-update) | async-done | bytes 147472 | tf_op jit(solution)/shard_map/psum | solution.py:101
  530.0 0.9 copy.10
  530.9 0.1 copy-done.8
  531.0 0.7 copy.11
  (28 shorter events, 0.2 us)
Async XLA Ops:
  14.2 14.7 %copy-start = (bf16[1,128,3072]{2,1,0:T(8,128)(2,1)S(1)}, bf16[1,128,3072]{2,1,0:T(8,128)(2,1)}, u32[]{:S(2)}) copy-start(bf16[1,128,3072]{2,1,0:T(8,128)(2,1)} %param.4) | copy-start | bytes 2359300
  14.2 173.2 %all-to-all-start = ((bf16[32,96,1536]{2,1,0:T(8,128)(2,1)}), bf16[32,96,1536]{2,1,0:T(8,128)(2,1)}, u32[]{:S(2)}, u32[]{:S(2)}) async-start(bf16[32,96,1536]{2,1,0:T(8,128)(2,1)} %bitcast.61), calls=%async_computation | async-start | bytes 18874368 | tf_op jit(solution)/shard_map/all_to_all | solution.py:67
  28.8 0.9 copy-start.9
  28.8 501.2 %all-reduce.2.cloned.1.call-start = ((), (), s32[]{:S(2)}) async-start(), calls=%async_computation.1 | async-start | bytes 294912 | tf_op jit(solution)/shard_map/psum | solution.py:101
  28.8 1.2 copy-start.1
  31.4 5.6 %collective-permute-start = (bf16[2,128,3072]{2,1,0:T(8,128)(2,1)}, bf16[2,128,3072]{2,1,0:T(8,128)(2,1)}, u32[]{:S(2)}, u32[]{:S(2)}) collective-permute-start(bf16[2,128,3072]{2,1,0:T(8,128)(2,1)} %pad_maximum_fusion.1), channel_id=1, source_target_pairs={{0,1},{1,0},{2,3},{3,2},{4,5},{5,4},{6,7},{7,6},{8,9},{9,8},{10,11... | collective-permute-start | bytes 4718600 | tf_op jit(solution)/shard_map/ppermute | solution.py:12
  38.7 1.2 copy-start.2
  38.7 1.7 copy-start.4
  40.3 1.2 copy-start.6
  187.3 9.5 %copy-start.5 = (bf16[2,128,3072]{2,1,0:T(8,128)(2,1)S(1)}, bf16[2,128,3072]{2,1,0:T(8,128)(2,1)}, u32[]{:S(2)}) copy-start(bf16[2,128,3072]{2,1,0:T(8,128)(2,1)} %copy-done.4) | copy-start | bytes 4718596
  187.3 9.5 %copy-start.7 = (bf16[1,256,3072]{2,1,0:T(8,128)(2,1)S(1)}, bf16[1,256,3072]{2,1,0:T(8,128)(2,1)}, u32[]{:S(2)}) copy-start(bf16[1,256,3072]{2,1,0:T(8,128)(2,1)} %copy-done.6) | copy-start | bytes 4718596
  192.9 3.9 copy-start.3
  193.1 9.7 %collective-permute-start.1 = (bf16[128,3072]{1,0:T(8,128)(2,1)S(1)}, bf16[128,3072]{1,0:T(8,128)(2,1)S(1)}, u32[]{:S(2)}, u32[]{:S(2)}) collective-permute-start(bf16[128,3072]{1,0:T(8,128)(2,1)S(1)} %select_convert_fusion), channel_id=1, source_target_pairs={{0,1},{1,0},{2,3},{3,2},{4,5},{5,4},{6,7},{7,6},{8,9},{9,8},{10,11... | collective-permute-start | bytes 2359304 | tf_op jit(solution)/shard_map/ppermute | solution.py:12
  204.5 21.0 %collective-permute-start.2 = (bf16[128,3072]{1,0:T(8,128)(2,1)S(1)}, bf16[128,3072]{1,0:T(8,128)(2,1)S(1)}, u32[]{:S(2)}, u32[]{:S(2)}) collective-permute-start(bf16[128,3072]{1,0:T(8,128)(2,1)S(1)} %fusion.12), channel_id=1, source_target_pairs={{32,0},{64,32},{96,64},{128,96},{160,128},{192,160},{224,192},{256... | collective-permute-start | bytes 2359304 | tf_op jit(solution)/shard_map/ppermute | solution.py:18
  530.0 1.0 copy-start.8
Sparse Core Ops, SparseCore 0:
  206.8 323.1 all-reduce.1
where the time goes:
time: 539 us
  waiting for transfers between devices  471 us (87%)
  starting transfers between devices  21.9 us (4%)
  between operations  14.3 us (3%)
  matrix products  13.3 us (2%)
  local copies, waits for them, and re-layouts  11.8 us (2%)
  other arithmetic  6.55 us (1%)
    psum x1, waiting for transfers between devices, on_device(): lax.psum(jnp.stack([grad_shift, grad_scale, gate_full], axis=1), 'shard')  304 us
    all_to_all x1, waiting for transfers between devices, on_device(): lax.all_to_all(outgoing, 'shard', split_axis=0, concat_axis=0, tiled=True)  144 us
    ppermute x1, waiting for transfers between devices, passed_along(): lax.ppermute(value, axis, [(source, source + steps) for source in range(l...  18.9 us
    all_to_all x1, starting transfers between devices, on_device(): lax.all_to_all(outgoing, 'shard', split_axis=0, concat_axis=0, tiled=True)  14.6 us
  transfers between devices with their start and end apart: 5, of which 4 were waited for; matrix products, arithmetic and copies ran while one was open for 2% of the time, Pallas kernels for 0%

commit v1 on v0

--- a/solution.py
+++ b/solution.py
@@ -98,7 +98,9 @@
         )
     grad_shift = sample_hot[:, None] * jnp.sum(current, axis=0)[None, :]
     grad_scale = sample_hot[:, None] * jnp.sum(current * normed, axis=0)[None, :]
-    totals = lax.psum(jnp.stack([grad_shift, grad_scale, gate_full], axis=1), "shard")
+    part = jnp.stack([grad_shift, grad_scale, gate_full], axis=1)
+    parts = lax.all_gather(part, "shard", axis=0, tiled=False)
+    totals = parts.sum(axis=0)
     grad_norm = current * (1.0 + own_mod[1])
     centered = grad_norm - jnp.mean(grad_norm, axis=-1, keepdims=True)
     grad_in = own_grad.astype(jnp.float32) + inv_scale * (

time: 539 us -> 345 us (0.64)
  waiting for transfers between devices: 471 us -> 272 us
    psum x1 -> x0, waiting for transfers between devices: 304 us -> none  [on_device(): lax.psum(jnp.stack([grad_shift, grad_scale, gate_full], axis=1), 'shard')]
    all_gather x0 -> x1, waiting for transfers between devices: none -> 105 us  [on_device(): parts = lax.all_gather(part, 'shard', axis=0, tiled=False)]
  transfers between devices with their start and end apart: 5 -> 5, of which waited for: 4 -> 4; matrix products, arithmetic and copies ran while one was open for 2% -> 4% of each run, Pallas kernels for 0% -> 0%
where the time goes in v1:
time: 345 us; the launch traced here: 344 us
  waiting for transfers between devices  272 us (79%)
  starting transfers between devices  21.9 us (6%)
  between operations  14.3 us (4%)
  matrix products  13.3 us (4%)
  local copies, waits for them, and re-layouts  12.5 us (4%)
  other arithmetic  9.94 us (3%)
    all_to_all x1, waiting for transfers between devices, on_device(): lax.all_to_all(outgoing, 'shard', split_axis=0, concat_axis=0, tiled=True)  144 us
    all_gather x1, waiting for transfers between devices, on_device(): parts = lax.all_gather(part, 'shard', axis=0, tiled=False)  105 us
    ppermute x1, waiting for transfers between devices, passed_along(): lax.ppermute(value, axis, [(source, source + steps) for source in range(l...  19.7 us
    all_to_all x1, starting transfers between devices, on_device(): lax.all_to_all(outgoing, 'shard', split_axis=0, concat_axis=0, tiled=True)  14.6 us
  transfers between devices with their start and end apart: 5, of which 4 were waited for; matrix products, arithmetic and copies ran while one was open for 4% of the time, Pallas kernels for 0%

profile of v1, /device:TPU:1, one launch (start us, length us, event | category | flops | bytes accessed | tf_op | source)
XLA Modules:
  0.0 344.3 jit_solution(9293381927958544892)
XLA Ops:
  7.2 2.2 reshape_squeeze.3
  9.4 4.7 %broadcast_in_dim.8 = bf16[16,2,96,1536]{3,2,1,0:T(8,128)(2,1)} broadcast(bf16[2,96,1536]{2,1,0:T(8,128)(2,1)S(1)} %copy.12), dimensions={1,2,3} | broadcast | bytes 10027008 | tf_op jit(solution)/shard_map/broadcast_in_dim | solution.py:63
  14.2 14.6 %all-to-all-start = ((bf16[32,96,1536]{2,1,0:T(8,128)(2,1)}), bf16[32,96,1536]{2,1,0:T(8,128)(2,1)}, u32[]{:S(2)}, u32[]{:S(2)}) async-start(bf16[32,96,1536]{2,1,0:T(8,128)(2,1)} %bitcast.61), calls=%async_computation | async-start | bytes 18874368 | tf_op jit(solution)/shard_map/all_to_all | solution.py:67
  28.9 0.2 convert_reduce_fusion
  29.1 0.4 fusion.14
  29.4 0.2 copy-done.8
  29.7 0.4 fusion.18
  30.1 1.3 pad_maximum_fusion.1
  31.4 2.2 collective-permute-start
  33.7 3.4 collective-permute-done
  37.0 1.6 broadcast_select_fusion.1
  38.7 0.3 pad_slice_fusion
  39.0 0.8 copy-done.2
  39.8 0.5 copy-done.4
  40.3 1.2 copy-done.6
  41.5 1.8 fusion
  43.4 144.0 %all-to-all-done = bf16[32,96,1536]{2,1,0:T(8,128)(2,1)} async-done(((bf16[32,96,1536]{2,1,0:T(8,128)(2,1)}), bf16[32,96,1536]{2,1,0:T(8,128)(2,1)}, u32[]{:S(2)}, u32[]{:S(2)}) %all-to-all-start) | async-done | bytes 9437216 | tf_op jit(solution)/shard_map/all_to_all | solution.py:67
  187.4 5.6 %fusion.29 = f32[256,3072]{1,0:T(8,128)S(1)} fusion(bf16[256,1536]{1,0:T(8,128)(2,1)} %fusion, bf16[3072,1536]{1,0:T(8,128)(2,1)} %bitcast.9), kind=kOutput, calls=%fused_computation.59 | convolution fusion | flops 2415919104 | bytes 13369344 | tf_op jit(solution)/shard_map/dot_general | solution.py:79
  192.9 0.1 select_convert_fusion
  193.1 3.7 %collective-permute-start.1 = (bf16[128,3072]{1,0:T(8,128)(2,1)S(1)}, bf16[128,3072]{1,0:T(8,128)(2,1)S(1)}, u32[]{:S(2)}, u32[]{:S(2)}) collective-permute-start(bf16[128,3072]{1,0:T(8,128)(2,1)S(1)} %select_convert_fusion), channel_id=1, source_target_pairs={{0,1},{1,0},{2,3},{3,2},{4,5},{5,4},{6,7},{7,6},{8,9},{9,8},{10,11... | collective-permute-start | bytes 2359304 | tf_op jit(solution)/shard_map/ppermute | solution.py:12
  196.9 5.2 %convolution_multiply_fusion = f32[256,1536]{1,0:T(8,128)S(1)} fusion(bf16[3072,1536]{1,0:T(8,128)(2,1)} %bitcast.9, bf16[2,128,3072]{2,1,0:T(8,128)(2,1)S(1)} %copy-done.5, bf16[2,128,3072]{2,1,0:T(8,128)(2,1)S(1)} %copy-done.3, bf16[1,256,3072]{2,1,0:T(8,128)(2,1)S(1)} %get-tuple-element.17, s32[]{:T(128)S(6)} %select_n.62, ...), kind=kOutput, calls=%fused_computation.2 | convolution fusion | flops 2421424128 | bytes 15728644 | tf_op jit(solution)/shard_map/dot_general | solution.py:77
  202.1 0.7 fusion.1
  202.8 0.9 fusion.13
  203.7 0.1 broadcast_multiply_fusion.1
  203.8 0.8 copy.13
  204.7 0.7 fusion.12
  205.4 1.3 collective-permute-start.2
  206.7 19.7 %collective-permute-done.2 = bf16[128,3072]{1,0:T(8,128)(2,1)S(1)} collective-permute-done((bf16[128,3072]{1,0:T(8,128)(2,1)S(1)}, bf16[128,3072]{1,0:T(8,128)(2,1)S(1)}, u32[]{:S(2)}, u32[]{:S(2)}) %collective-permute-start.2) | collective-permute-done | bytes 786464 | tf_op jit(solution)/shard_map/ppermute | solution.py:18
  226.4 105.3 %all-gather.3.cloned.1.call-done = f32[128,3,3072]{2,1,0:T(4,128)} async-done(((f32[4,3,3072]{2,1,0:T(4,128)}), f32[128,3,3072]{2,1,0:T(4,128)}) %all-gather.3.cloned.1.call-update) | async-done | bytes 4718608 | tf_op jit(solution)/shard_map/all_gather | solution.py:102
  331.7 4.2 %reduce_sum.69 = f32[4,3,3072]{2,1,0:T(4,128)S(1)} reduce(f32[32,4,3,3072]{3,2,1,0:T(4,128)} %bitcast.62, f32[]{:T(128)} %constant.71.clone.1), dimensions={0}, to_apply=%region_6.7 | reduce | flops 1142784 | bytes 4866052 | tf_op jit(solution)/shard_map/reduce_sum | solution.py:103
  335.8 0.8 copy.14
  336.6 0.9 copy.17
  (28 shorter events, 0.3 us)
Async XLA Ops:
  14.2 14.7 %copy-start = (bf16[1,128,3072]{2,1,0:T(8,128)(2,1)S(1)}, bf16[1,128,3072]{2,1,0:T(8,128)(2,1)}, u32[]{:S(2)}) copy-start(bf16[1,128,3072]{2,1,0:T(8,128)(2,1)} %param.4) | copy-start | bytes 2359300
  14.2 173.2 %all-to-all-start = ((bf16[32,96,1536]{2,1,0:T(8,128)(2,1)}), bf16[32,96,1536]{2,1,0:T(8,128)(2,1)}, u32[]{:S(2)}, u32[]{:S(2)}) async-start(bf16[32,96,1536]{2,1,0:T(8,128)(2,1)} %bitcast.61), calls=%async_computation | async-start | bytes 18874368 | tf_op jit(solution)/shard_map/all_to_all | solution.py:67
  28.8 0.9 copy-start.8
  28.8 302.9 %all-gather.3.cloned.1.call-start = ((), (), s32[]{:S(2)}) async-start(), calls=%async_computation.1 | async-start | bytes 6488064 | tf_op jit(solution)/shard_map/all_gather | solution.py:102
  28.9 1.2 copy-start.1
  31.4 5.6 %collective-permute-start = (bf16[2,128,3072]{2,1,0:T(8,128)(2,1)}, bf16[2,128,3072]{2,1,0:T(8,128)(2,1)}, u32[]{:S(2)}, u32[]{:S(2)}) collective-permute-start(bf16[2,128,3072]{2,1,0:T(8,128)(2,1)} %pad_maximum_fusion.1), channel_id=1, source_target_pairs={{0,1},{1,0},{2,3},{3,2},{4,5},{5,4},{6,7},{7,6},{8,9},{9,8},{10,11... | collective-permute-start | bytes 4718600 | tf_op jit(solution)/shard_map/ppermute | solution.py:12
  38.6 1.2 copy-start.2
  38.7 1.7 copy-start.4
  40.3 1.2 copy-start.6
  187.4 9.5 %copy-start.5 = (bf16[2,128,3072]{2,1,0:T(8,128)(2,1)S(1)}, bf16[2,128,3072]{2,1,0:T(8,128)(2,1)}, u32[]{:S(2)}) copy-start(bf16[2,128,3072]{2,1,0:T(8,128)(2,1)} %copy-done.4) | copy-start | bytes 4718596
  187.4 9.5 %copy-start.7 = (bf16[1,256,3072]{2,1,0:T(8,128)(2,1)S(1)}, bf16[1,256,3072]{2,1,0:T(8,128)(2,1)}, u32[]{:S(2)}) copy-start(bf16[1,256,3072]{2,1,0:T(8,128)(2,1)} %copy-done.6) | copy-start | bytes 4718596
  192.9 3.9 %copy-start.3 = (bf16[2,128,3072]{2,1,0:T(8,128)(2,1)S(1)}, bf16[2,128,3072]{2,1,0:T(8,128)(2,1)}, u32[]{:S(2)}) copy-start(bf16[2,128,3072]{2,1,0:T(8,128)(2,1)} %copy-done.2) | copy-start | bytes 4718596
  193.1 9.7 %collective-permute-start.1 = (bf16[128,3072]{1,0:T(8,128)(2,1)S(1)}, bf16[128,3072]{1,0:T(8,128)(2,1)S(1)}, u32[]{:S(2)}, u32[]{:S(2)}) collective-permute-start(bf16[128,3072]{1,0:T(8,128)(2,1)S(1)} %select_convert_fusion), channel_id=1, source_target_pairs={{0,1},{1,0},{2,3},{3,2},{4,5},{5,4},{6,7},{7,6},{8,9},{9,8},{10,11... | collective-permute-start | bytes 2359304 | tf_op jit(solution)/shard_map/ppermute | solution.py:12
  205.4 21.0 %collective-permute-start.2 = (bf16[128,3072]{1,0:T(8,128)(2,1)S(1)}, bf16[128,3072]{1,0:T(8,128)(2,1)S(1)}, u32[]{:S(2)}, u32[]{:S(2)}) collective-permute-start(bf16[128,3072]{1,0:T(8,128)(2,1)S(1)} %fusion.12), channel_id=1, source_target_pairs={{32,0},{64,32},{96,64},{128,96},{160,128},{192,160},{224,192},{256... | collective-permute-start | bytes 2359304 | tf_op jit(solution)/shard_map/ppermute | solution.py:18
Sparse Core Ops, SparseCore 0:
  204.8 126.8 all-gather.2
